TPU v7x, 32 devices: a whole 2x2x4 slice. The times are simulated.
32 devices in a mesh: dp: 8 (over z, core), chan: 4 (over y, x).
Axes of the slice: x: 2, y: 2, z: 4, core: 2. Of those that a mesh axis runs over, the one named last changes fastest.
Arguments:
- images: bfloat16 [16, 16, 16, 2816], P('dp', None, None, 'chan'), may hold values from -6 to 6
- kernel: float32 [7, 7, 2816], P(None, None, 'chan'), may hold values from -0.875 to 0.875
- layernorm_gain: float32 [2816], P('chan'), may hold values from 0.25 to 1.75
- layernorm_bias: float32 [2816], P('chan'), may hold values from -3 to 3
- w_expand: bfloat16 [2816, 11264], P('dp', 'chan'), may hold values from -0.109375 to 0.109375
- w_reduce: bfloat16 [11264, 2816], P('chan', 'dp'), may hold values from -0.0546875 to 0.0546875
- layer_scale: float32 [2816], P('chan'), may hold values from 0.25 to 1
- cotangent: bfloat16 [16, 16, 16, 2816], P('dp', None, None, 'chan'), may hold values from -6 to 6
Outputs:
- output: bfloat16 [16, 16, 16, 2816], P('dp', None, None, 'chan')
- grad_images: bfloat16 [16, 16, 16, 2816], P('dp', None, None, 'chan')
- grad_kernel: float32 [7, 7, 2816], P(None, None, 'chan')
- gain_gradient: float32 [2816], P('chan')
- grad_bias: float32 [2816], P('chan')
- grad_expand: float32 [2816, 11264], P('dp', 'chan')
- grad_reduce: float32 [11264, 2816], P('chan', 'dp')
- grad_scale: float32 [2816], P('chan')
All inputs are finite; a program needn't handle non-finite values.
Results may differ from a plain program's by a relative error of at most 0.025.
Values may be sent and summed in bfloat16 or wider, within the bound.
A program may use at most 128 MiB of HBM per device.

v0:
```python
import math
import jax
import jax.numpy as jnp
from jax import lax
from jax.sharding import PartitionSpec as P

eps = 1e-06


def depthwise(field, kern):
    height = field.shape[1]
    breadth = field.shape[2]
    padded = jnp.pad(field, ((0, 0), (3, 3), (3, 3), (0, 0)))
    total = jnp.zeros(field.shape, jnp.float32)
    for i in range(7):
        for j in range(7):
            total = total + padded[:, i : i + height, j : j + breadth, :] * kern[i, j]
    return total


def normal_cdf(value):
    return 0.5 * (1.0 + jax.scipy.special.erf(value / math.sqrt(2.0)))


def swap_pairs(shift, n):
    return [(i, i ^ shift) for i in range(n)]


def chan_gather(block):
    n = lax.axis_size("chan")
    me = lax.axis_index("chan")
    width = block.shape[1]
    whole = jnp.zeros((block.shape[0], n * width), block.dtype)
    parts = [block] + [lax.ppermute(block, "chan", swap_pairs(k, n)) for k in range(1, n)]
    for k in range(n):
        whole = lax.dynamic_update_slice(whole, parts[k], (0, (me ^ k) * width))
    return whole


def chan_scatter(partial):
    n = lax.axis_size("chan")
    me = lax.axis_index("chan")
    width = partial.shape[1] // n
    total = lax.dynamic_slice_in_dim(partial, me * width, width, 1).astype(jnp.float32)
    for k in range(1, n):
        mine = lax.dynamic_slice_in_dim(partial, (me ^ k) * width, width, 1)
        total = total + lax.ppermute(mine, "chan", swap_pairs(k, n)).astype(jnp.float32)
    return total


def dp_scatter(partial):
    return lax.psum_scatter(partial, "dp", scatter_dimension=0, tiled=True)


def dp_line_scatter(partial, early):
    n = lax.axis_size("dp")
    m = n // 2
    me = lax.axis_index("dp")
    place, side = (me // 2, me % 2)
    blocks = partial.reshape(m, 2, partial.shape[0] // n, partial.shape[1])
    own = lax.dynamic_index_in_dim(blocks, side, 1, keepdims=False)
    other = lax.dynamic_index_in_dim(blocks, 1 - side, 1, keepdims=False)
    own = own + lax.ppermute(other, "dp", swap_pairs(1, n))
    up = down = None
    for distance in range(m - 1, 0, -1):
        high = lax.dynamic_index_in_dim(
            own, jnp.minimum(place + distance, m - 1), 0, keepdims=False
        )
        low = lax.dynamic_index_in_dim(own, jnp.maximum(place - distance, 0), 0, keepdims=False)
        if up is not None:
            high, low = (high + up, low + down)
        senders = range(2 * (m - distance))
        up = lax.ppermute(high, "dp", [(i, i + 2) for i in senders])
        down = lax.ppermute(low, "dp", [(n - 1 - i, n - 3 - i) for i in senders])
        if distance == 2:
            up, down, early = lax.optimization_barrier((up, down, early))
    mine = lax.dynamic_index_in_dim(own, place, 0, keepdims=False).astype(jnp.float32)
    return (mine + up.astype(jnp.float32) + down.astype(jnp.float32), early)


def dp_total(value):
    n = lax.axis_size("dp")
    shift = 1
    while shift < n:
        value = value + lax.ppermute(value, "dp", swap_pairs(shift, n))
        shift *= 2
    return value


def body(
    images, kernel, layernorm_gain, layernorm_bias, w_expand, w_reduce, layer_scale, cotangent
):
    shape_in = images.shape
    height = shape_in[1]
    breadth = shape_in[2]
    positions = shape_in[0] * height * breadth
    local_chan = shape_in[3]
    image_width = local_chan * lax.axis_size("chan")
    xf = images.astype(jnp.float32)
    conv = depthwise(xf, kernel).reshape(positions, local_chan)
    mean_val = lax.psum(jnp.sum(conv, axis=1), "chan")[:, None] / image_width
    centred_rows = conv - mean_val
    var = lax.psum(jnp.sum(centred_rows * centred_rows, axis=1), "chan")[:, None] / image_width
    inverse_deviation = lax.rsqrt(var + eps)
    standardized_input = centred_rows * inverse_deviation
    normed_output = (standardized_input * layernorm_gain + layernorm_bias).astype(jnp.bfloat16)
    normed_all = chan_gather(normed_output)
    expand_all = lax.all_gather(w_expand, "dp", axis=0, tiled=True)
    pre = jnp.dot(normed_all, expand_all, preferred_element_type=jnp.float32)
    hidden = (pre * normal_cdf(pre)).astype(jnp.bfloat16)
    dyf = cotangent.astype(jnp.float32).reshape(positions, local_chan)
    dbranch = (dyf * layer_scale).astype(jnp.bfloat16)
    dbranch_all = chan_gather(dbranch)
    reduce_part = lax.dot_general(
        dbranch_all, hidden, (((0,), (0,)), ((), ())), preferred_element_type=jnp.float32
    ).astype(jnp.bfloat16)
    reduce_all = lax.all_gather(w_reduce, "dp", axis=1, tiled=True)
    grad_reduce, reduce_all = dp_line_scatter(reduce_part, reduce_all)
    grad_reduce = grad_reduce.T
    dhidden = lax.dot_general(
        dbranch_all, reduce_all, (((1,), (1,)), ((), ())), preferred_element_type=jnp.float32
    )
    slope = normal_cdf(pre) + pre * jnp.exp(-0.5 * pre * pre) / math.sqrt(2.0 * math.pi)
    dpre = (dhidden * slope).astype(jnp.bfloat16)
    expand_part = lax.dot_general(
        normed_all, dpre, (((0,), (0,)), ((), ())), preferred_element_type=jnp.float32
    ).astype(jnp.bfloat16)
    expand_part, dpre, hidden, reduce_all = lax.optimization_barrier(
        (expand_part, dpre, hidden, reduce_all)
    )
    grad_expand = dp_scatter(expand_part).astype(jnp.float32)
    partial_normed = lax.dot_general(
        dpre, expand_all, (((1,), (1,)), ((), ())), preferred_element_type=jnp.float32
    )
    normed_grad = chan_scatter(partial_normed.astype(jnp.bfloat16))
    partial_branch = jnp.dot(hidden, reduce_all, preferred_element_type=jnp.float32)
    branch = chan_scatter(partial_branch.astype(jnp.bfloat16))
    xr = xf.reshape(positions, local_chan)
    output = (xr + layer_scale * branch).astype(jnp.bfloat16).reshape(shape_in)
    scale_part = jnp.sum(dyf * branch, axis=0)
    gain_partial = jnp.sum(normed_grad * standardized_input, axis=0)
    bias_part = jnp.sum(normed_grad, axis=0)
    standardized_grad = normed_grad * layernorm_gain
    first_half, second_half = lax.psum(
        (
            jnp.sum(standardized_grad, axis=1),
            jnp.sum(standardized_grad * standardized_input, axis=1),
        ),
        "chan",
    )
    conv_output_grad = inverse_deviation * (
        standardized_grad
        - first_half[:, None] / image_width
        - standardized_input * (second_half[:, None] / image_width)
    )
    conv_output_grad = conv_output_grad.reshape(shape_in)
    padded = jnp.pad(xf, ((0, 0), (3, 3), (3, 3), (0, 0)))
    dpad = jnp.pad(conv_output_grad, ((0, 0), (3, 3), (3, 3), (0, 0)))
    back = cotangent.astype(jnp.float32)
    kern_rows = []
    for i in range(7):
        tap_row = []
        for j in range(7):
            tap_row.append(
                jnp.sum(
                    padded[:, i : i + height, j : j + breadth, :] * conv_output_grad, axis=(0, 1, 2)
                )
            )
            back = back + dpad[:, 6 - i : 6 - i + height, 6 - j : 6 - j + breadth, :] * kernel[i, j]
        kern_rows.append(jnp.stack(tap_row))
    kernel_part = jnp.stack(kern_rows)
    grad_images = back.astype(jnp.bfloat16)
    small = dp_total(
        jnp.concatenate(
            [
                kernel_part.reshape(-1, local_chan),
                gain_partial[None],
                bias_part[None],
                scale_part[None],
            ]
        )
    )
    taps = kernel_part.shape[0] * kernel_part.shape[1]
    grad_kernel = small[:taps].reshape(kernel_part.shape)
    gain_gradient, grad_bias, grad_scale = (small[taps], small[taps + 1], small[taps + 2])
    return (
        output,
        grad_images,
        grad_kernel,
        gain_gradient,
        grad_bias,
        grad_expand,
        grad_reduce,
        grad_scale,
    )


def solution(mesh):
    in_specs = (
        P("dp", None, None, "chan"),
        P(None, None, "chan"),
        P("chan"),
        P("chan"),
        P("dp", "chan"),
        P("chan", "dp"),
        P("chan"),
        P("dp", None, None, "chan"),
    )
    out_specs = (
        P("dp", None, None, "chan"),
        P("dp", None, None, "chan"),
        P(None, None, "chan"),
        P("chan"),
        P("chan"),
        P("dp", "chan"),
        P("chan", "dp"),
        P("chan"),
    )
    return jax.shard_map(body, mesh=mesh, in_specs=in_specs, out_specs=out_specs, check_vma=False)
```

profile of v0, /device:TPU:0, one launch (start us, length us, event | category | flops | bytes accessed | tf_op | source)
XLA Modules:
  0.0 646.5 jit_solution(1714485748534928411)
XLA Ops:
  11.0 13.1 %fusion.110 = (f32[2,16,16]{2,1,0:T(8,128)S(1)}, f32[2,16,16,704]{3,2,1,0:T(8,128)S(1)}) fusion(f32[704]{0:T(1024)S(1)} %get-tuple-element.125, f32[704]{0:T(1024)S(1)} %get-tuple-element.126, f32[704]{0:T(1024)S(1)} %get-tuple-element.79, f32[704]{0:T(1024)S(1)} %get-tuple-element.80, f32[704]{0:T(1024)S(1)} %get-tuple-element.81, ...), kind=kLoop, calls=%fused_computation.354 | loop fusion | flops 35323392 | bytes 3023616 | tf_op jit(solution)/shard_map/reduce_sum | solution.py:101
  24.6 11.3 %psum.28 = f32[512]{0:T(512)S(1)} all-reduce(f32[512]{0:T(512)S(1)} %reduce_sum.509), channel_id=1, replica_groups=mesh['dp'=8,'chan'=4] {'chan'}, use_global_device_ids=true, to_apply=%region_1.2 | all-reduce | flops 512 | bytes 4096 | tf_op jit(solution)/shard_map/psum | solution.py:101
  36.4 8.5 %psum.29 = f32[512]{0:T(512)S(1)} all-reduce(f32[512]{0:T(512)S(1)} %reduce_sum.511), channel_id=1, replica_groups=mesh['dp'=8,'chan'=4] {'chan'}, use_global_device_ids=true, to_apply=%region_3.4 | all-reduce | flops 512 | bytes 4096 | tf_op jit(solution)/shard_map/psum | solution.py:103
  46.4 1.5 collective-permute-start
  51.8 1.5 collective-permute-start.2
  53.3 12.5 %collective-permute-done = bf16[512,704]{0,1:T(8,128)(2,1)} collective-permute-done((bf16[512,704]{0,1:T(8,128)(2,1)}, bf16[512,704]{0,1:T(8,128)(2,1)}, u32[]{:S(2)}, u32[]{:S(2)}) %collective-permute-start) | collective-permute-done | bytes 720928 | tf_op jit(solution)/shard_map/ppermute | solution.py:34
  65.8 1.5 collective-permute-start.5
  67.4 1.8 broadcast.41.clone
  69.1 7.8 %dynamic_update_slice.24 = bf16[512,2816]{1,0:T(8,128)(2,1)} dynamic-update-slice(bf16[512,2816]{1,0:T(8,128)(2,1)} %broadcast.41.clone, bf16[512,704]{1,0:T(8,128)(2,1)S(1)} %copy-done.10, s32[]{:T(128)} %constant.80.clone.1, s32[]{:T(128)S(6)} %select_n.58) | dynamic-update-slice | bytes 1441796 | tf_op jit(solution)/shard_map/dynamic_update_slice | solution.py:36
  76.9 1.8 broadcast.41.clone.1
  78.7 7.9 %dynamic_update_slice.28 = bf16[512,2816]{1,0:T(8,128)(2,1)} dynamic-update-slice(bf16[512,2816]{1,0:T(8,128)(2,1)} %broadcast.41.clone.1, bf16[512,704]{1,0:T(8,128)(2,1)S(1)} %fusion.106, s32[]{:T(128)} %constant.80.clone.1, s32[]{:T(128)S(6)} %select_n.58) | dynamic-update-slice | bytes 1441796 | tf_op jit(solution)/shard_map/dynamic_update_slice | solution.py:36
  88.0 8.7 %dynamic_update_slice.25 = bf16[512,2816]{1,0:T(8,128)(2,1)} dynamic-update-slice(bf16[512,2816]{1,0:T(8,128)(2,1)} %dynamic_update_slice.24, bf16[512,704]{1,0:T(8,128)(2,1)S(1)} %copy.17, s32[]{:T(128)} %constant.80.clone.1, s32[]{:T(128)S(6)} %select_n.59) | dynamic-update-slice | bytes 1441796 | tf_op jit(solution)/shard_map/dynamic_update_slice | solution.py:36
  98.0 8.7 %dynamic_update_slice.29 = bf16[512,2816]{1,0:T(8,128)(2,1)} dynamic-update-slice(bf16[512,2816]{1,0:T(8,128)(2,1)} %dynamic_update_slice.28, bf16[512,704]{1,0:T(8,128)(2,1)S(1)} %copy.23, s32[]{:T(128)} %constant.80.clone.1, s32[]{:T(128)S(6)} %select_n.59) | dynamic-update-slice | bytes 1441796 | tf_op jit(solution)/shard_map/dynamic_update_slice | solution.py:36
  108.1 7.8 %dynamic_update_slice.26 = bf16[512,2816]{1,0:T(8,128)(2,1)} dynamic-update-slice(bf16[512,2816]{1,0:T(8,128)(2,1)} %dynamic_update_slice.25, bf16[512,704]{1,0:T(8,128)(2,1)S(1)} %copy.19, s32[]{:T(128)} %constant.80.clone.1, s32[]{:T(128)S(6)} %select_n.60) | dynamic-update-slice | bytes 1441796 | tf_op jit(solution)/shard_map/dynamic_update_slice | solution.py:36
  117.3 7.8 %dynamic_update_slice.30 = bf16[512,2816]{1,0:T(8,128)(2,1)} dynamic-update-slice(bf16[512,2816]{1,0:T(8,128)(2,1)} %dynamic_update_slice.29, bf16[512,704]{1,0:T(8,128)(2,1)S(1)} %copy.25, s32[]{:T(128)} %constant.80.clone.1, s32[]{:T(128)S(6)} %select_n.60) | dynamic-update-slice | bytes 1441796 | tf_op jit(solution)/shard_map/dynamic_update_slice | solution.py:36
  126.5 8.0 %dynamic_update_slice.27 = bf16[512,2816]{1,0:T(8,128)(2,1)} dynamic-update-slice(bf16[512,2816]{1,0:T(8,128)(2,1)} %dynamic_update_slice.26, bf16[512,704]{1,0:T(8,128)(2,1)S(1)} %copy.21, s32[]{:T(128)} %constant.80.clone.1, s32[]{:T(128)S(6)} %select_n.61) | dynamic-update-slice | bytes 1441796 | tf_op jit(solution)/shard_map/dynamic_update_slice | solution.py:36
  135.8 8.0 %dynamic_update_slice.31 = bf16[512,2816]{1,0:T(8,128)(2,1)} dynamic-update-slice(bf16[512,2816]{1,0:T(8,128)(2,1)} %dynamic_update_slice.30, bf16[512,704]{1,0:T(8,128)(2,1)S(1)} %copy.27, s32[]{:T(128)} %constant.80.clone.1, s32[]{:T(128)S(6)} %select_n.61) | dynamic-update-slice | bytes 1441796 | tf_op jit(solution)/shard_map/dynamic_update_slice | solution.py:36
  143.8 12.2 %all-gather.3.cloned.1.call-done = bf16[2816,2816]{1,0:T(8,128)(2,1)} async-done(((bf16[352,2816]{1,0:T(8,128)(2,1)}), bf16[2816,2816]{1,0:T(8,128)(2,1)}) %all-gather.3.cloned.1.call-update) | async-done | bytes 15859728 | tf_op jit(solution)/shard_map/all_gather | solution.py:108
  156.0 15.2 %multiply_convert_fusion = (bf16[512,2816]{1,0:T(8,128)(2,1)S(1)}, f32[512,2816]{1,0:T(8,128)}) fusion(bf16[512,2816]{1,0:T(8,128)(2,1)} %dynamic_update_slice.27, bf16[2816,2816]{1,0:T(8,128)(2,1)} %all-gather.3.cloned.1.call-done), kind=kOutput, calls=%fused_computation.107 | convolution fusion | flops 8127381504 | bytes 27394048 | tf_op jit(solution)/shard_map/dot_general | solution.py:109
  171.2 12.0 %convolution_convert_fusion.1 = bf16[2816,2816]{1,0:T(8,128)(2,1)} fusion(bf16[512,2816]{1,0:T(8,128)(2,1)S(1)} %copy-done.13, bf16[512,2816]{1,0:T(8,128)(2,1)S(1)} %get-tuple-element.16), kind=kOutput, calls=%fused_computation.97 | convolution fusion | flops 8128102400 | bytes 21626880 | tf_op jit(solution)/shard_map/dot_general | solution.py:114
  183.2 7.0 %dynamic-slice_bitcast_fusion = bf16[4,352,2816]{2,1,0:T(8,128)(2,1)} fusion(bf16[4,2,352,2816]{3,2,1,0:T(8,128)(2,1)} %bitcast.125, s32[]{:T(128)S(6)} %select_n.64), kind=kLoop, calls=%fused_computation.100 | loop fusion | bytes 15859716 | tf_op jit(solution)/shard_map/jit(dynamic_index_in_dim)/squeeze | solution.py:62
  190.4 12.7 %collective-permute-done.6 = bf16[4,352,2816]{2,1,0:T(8,128)(2,1)} collective-permute-done((bf16[4,352,2816]{2,1,0:T(8,128)(2,1)}, bf16[4,352,2816]{2,1,0:T(8,128)(2,1)}, u32[]{:S(2)}, u32[]{:S(2)}) %collective-permute-start.6) | collective-permute-done | bytes 7929888 | tf_op jit(solution)/shard_map/ppermute | solution.py:63
  203.1 6.2 bitcast_add_fusion
  209.4 2.4 dynamic-slice_bitcast_fusion.1
  211.8 2.0 copy-done
  215.2 2.0 collective-permute-start.9
  217.2 84.0 %collective-permute-done.7 = bf16[352,2816]{1,0:T(8,128)(2,1)S(1)} collective-permute-done((bf16[352,2816]{1,0:T(8,128)(2,1)}, bf16[352,2816]{1,0:T(8,128)(2,1)S(1)}, u32[]{:S(2)}, u32[]{:S(2)}) %collective-permute-start.7) | collective-permute-done | bytes 1982496 | tf_op jit(solution)/shard_map/ppermute | solution.py:73
  301.2 5.2 bitcast_add_fusion.3
  307.2 6.1 collective-permute-start.8
  313.2 46.3 %all-gather.5.cloned.1.call-done = bf16[2816,2816]{0,1:T(8,128)(2,1)} async-done(((bf16[2816,352]{0,1:T(8,128)(2,1)}), bf16[2816,2816]{0,1:T(8,128)(2,1)}) %all-gather.5.cloned.1.call-update) | async-done | bytes 15859728 | tf_op jit(solution)/shard_map/all_gather | solution.py:117
  359.6 18.9 %collective-permute-done.8 = bf16[352,2816]{1,0:T(8,128)(2,1)} collective-permute-done((bf16[352,2816]{1,0:T(8,128)(2,1)}, bf16[352,2816]{1,0:T(8,128)(2,1)}, u32[]{:S(2)}, u32[]{:S(2)}) %collective-permute-start.8) | collective-permute-done | bytes 1982496 | tf_op jit(solution)/shard_map/ppermute | solution.py:73
  378.5 15.5 %fusion.5 = bf16[512,2816]{1,0:T(8,128)(2,1)S(1)} fusion(f32[512,2816]{1,0:T(8,128)} %get-tuple-element.148, bf16[512,2816]{1,0:T(8,128)(2,1)} %dynamic_update_slice.31, bf16[2816,2816]{0,1:T(8,128)(2,1)} %all-gather.5.cloned.1.call-done), kind=kOutput, calls=%fused_computation.106 | convolution fusion | flops 8134590464 | bytes 27394048 | tf_op jit(solution)/shard_map/dot_general | solution.py:120
  394.0 1.5 copy-done.103
  395.5 11.8 %convolution_convert_fusion = bf16[2816,2816]{1,0:T(8,128)(2,1)} fusion(bf16[512,2816]{1,0:T(8,128)(2,1)S(1)} %copy-done.14, bf16[512,2816]{1,0:T(8,128)(2,1)S(1)} %fusion.5), kind=kOutput, calls=%fused_computation.96 | convolution fusion | flops 8128102400 | bytes 21626880 | tf_op jit(solution)/shard_map/dot_general | solution.py:125
  407.4 13.8 %convolution_convert_fusion.2 = bf16[512,2816]{1,0:T(8,128)(2,1)S(1)} fusion(bf16[512,2816]{1,0:T(8,128)(2,1)} %copy-done.103, bf16[2816,2816]{1,0:T(8,128)(2,1)} %all-gather.3.cloned.1.call-done), kind=kOutput, calls=%fused_computation.109 | convolution fusion | flops 8121614336 | bytes 21626880 | tf_op jit(solution)/shard_map/dot_general | solution.py:132
  421.2 2.2 constant_dynamic-slice_fusion.2
  423.4 2.3 copy.34
  425.7 1.7 collective-permute-start.14
  428.6 1.5 collective-permute-start.15
  431.5 13.5 %convolution_convert_fusion.3 = bf16[512,2816]{1,0:T(8,128)(2,1)S(1)} fusion(bf16[512,2816]{1,0:T(8,128)(2,1)} %copy-done.102, bf16[2816,2816]{0,1:T(8,128)(2,1)} %all-gather.5.cloned.1.call-done), kind=kOutput, calls=%fused_computation.110 | convolution fusion | flops 8121614336 | bytes 21626880 | tf_op jit(solution)/shard_map/dot_general | solution.py:136
  445.1 2.2 constant_dynamic-slice_fusion.5
  447.3 2.3 copy.28
  449.6 1.7 collective-permute-start.11
  452.4 1.5 collective-permute-start.12
  455.3 2.3 copy.35
  457.6 5.5 collective-permute-done.15
  463.1 2.3 copy.37
  465.5 2.3 copy.39
  467.8 8.3 %collective-permute-done.11 = bf16[512,704]{0,1:T(8,128)(2,1)} collective-permute-done((bf16[512,704]{0,1:T(8,128)(2,1)}, bf16[512,704]{0,1:T(8,128)(2,1)}, u32[]{:S(2)}, u32[]{:S(2)}) %collective-permute-start.11) | collective-permute-done | bytes 720928 | tf_op jit(solution)/shard_map/ppermute | solution.py:47
  476.0 2.3 copy.29
  478.4 14.3 %collective-permute-done.12 = bf16[512,704]{0,1:T(8,128)(2,1)S(1)} collective-permute-done((bf16[512,704]{0,1:T(8,128)(2,1)}, bf16[512,704]{0,1:T(8,128)(2,1)S(1)}, u32[]{:S(2)}, u32[]{:S(2)}) %collective-permute-start.12) | collective-permute-done | bytes 720928 | tf_op jit(solution)/shard_map/ppermute | solution.py:47
  495.0 5.6 fusion.107
  500.6 9.1 %all-reduce.2 = (f32[512]{0:T(512)S(1)}, f32[512]{0:T(512)S(1)}) all-reduce(f32[512]{0:T(512)S(1)} %get-tuple-element.151, f32[512]{0:T(512)S(1)} %get-tuple-element.150), channel_id=1, replica_groups=mesh['dp'=8,'chan'=4] {'chan'}, use_global_device_ids=true, to_apply=%region_7.8 | all-reduce | flops 1024 | bytes 8192 | tf_op jit(solution)/shard_map/psum | solution.py:144
  509.8 6.5 %multiply_reduce_fusion.2 = (f32[704]{0:T(1024)S(1)}, f32[704]{0:T(1024)S(1)}, f32[704]{0:T(1024)S(1)}, f32[704]{0:T(1024)S(1)}, f32[704]{0:T(1024)S(1)}, /*inde...) fusion(f32[2,16,16,704]{3,2,1,0:T(8,128)S(1)} %copy-done.2, ...), kind=kLoop, calls=%fused_computation.228 | loop fusion | flops 15486592 | bytes 5828864 | tf_op jit(solution)/shard_map/reduce_sum | solution.py:165
  516.3 4.1 multiply_reduce_fusion.1
  520.4 2.8 multiply_reduce_fusion.3
  524.9 5.8 bitcast_add_fusion.2
  530.7 5.5 collective-permute-start.20
  537.6 2.7 collective-permute-start.18
  540.3 73.3 %collective-permute-done.18 = f32[52,704]{1,0:T(8,128)S(1)} collective-permute-done((f32[52,704]{1,0:T(8,128)S(1)}, f32[52,704]{1,0:T(8,128)S(1)}, u32[]{:S(2)}, u32[]{:S(2)}) %collective-permute-start.18) | collective-permute-done | bytes 146464 | tf_op jit(solution)/shard_map/ppermute | solution.py:85
  613.6 2.1 collective-permute-start.19
  616.0 13.3 %fusion.101 = bf16[2,16,16,704]{3,2,1,0:T(8,128)(2,1)} fusion(f32[2,16,16,704]{3,2,1,0:T(8,128)S(1)} %bitcast.124, bf16[2,16,16,704]{3,2,1,0:T(8,128)(2,1)S(1)} %copy-done.6, f32[704]{0:T(1024)S(1)} %copy-done.40, f32[704]{0:T(1024)S(1)} %copy-done.42, f32[704]{0:T(1024)S(1)} %copy-done.46, f32[704]{0:T(1024)S(1)} %copy-done.48, f32[704]{0:T(1024)S(1)} %copy-done.50, ...), kind=kLoop, calls=%fused_computation.213 | loop fusion | flops 36044800 | bytes 3021568 | tf_op jit(solution)/shard_map/convert_element_type | solution.py:172
  630.7 5.3 fusion.7
  636.0 3.7 convert_element_type.100
  (338 shorter events, 31.4 us)
Async XLA Ops:
  7.2 148.8 %all-gather.3.cloned.1.call-start = ((), (), s32[]{:S(2)}) async-start(), calls=%async_computation.1 | async-start | bytes 17842176 | tf_op jit(solution)/shard_map/all_gather | solution.py:108
  7.9 351.7 %all-gather.5.cloned.1.call-start = ((), (), s32[]{:S(2)}) async-start(), calls=%async_computation.2 | async-start | bytes 17842176 | tf_op jit(solution)/shard_map/all_gather | solution.py:117
  8.7 627.3 %reduce-scatter.2.cloned.1.call-start = ((), (), s32[]{:S(2)}) async-start(), calls=%async_computation.3 | async-start | bytes 17842176 | tf_op jit(solution)/shard_map/reduce_scatter | solution.py:52
  46.4 19.4 %collective-permute-start = (bf16[512,704]{0,1:T(8,128)(2,1)}, bf16[512,704]{0,1:T(8,128)(2,1)}, u32[]{:S(2)}, u32[]{:S(2)}) collective-permute-start(bf16[512,704]{0,1:T(8,128)(2,1)} %copy.16), channel_id=1, source_target_pairs={{0,1},{1,0},{2,3},{3,2},{4,5},{5,4},{6,7},{7,6},{8,9},{9,8},{10,11... | collective-permute-start | bytes 2162696 | tf_op jit(solution)/shard_map/ppermute | solution.py:34
  49.2 47.4 %collective-permute-start.3 = (bf16[512,704]{0,1:T(8,128)(2,1)}, bf16[512,704]{0,1:T(8,128)(2,1)}, u32[]{:S(2)}, u32[]{:S(2)}) collective-permute-start(bf16[512,704]{0,1:T(8,128)(2,1)} %copy.22), channel_id=1, source_target_pairs={{0,1},{1,0},{2,3},{3,2},{4,5},{5,4},{6,7},{7,6},{8,9},{9,8},{10,11... | collective-permute-start | bytes 2162696 | tf_op jit(solution)/shard_map/ppermute | solution.py:34
  49.7 57.0 %collective-permute-start.1 = (bf16[512,704]{0,1:T(8,128)(2,1)}, bf16[512,704]{0,1:T(8,128)(2,1)}, u32[]{:S(2)}, u32[]{:S(2)}) collective-permute-start(bf16[512,704]{0,1:T(8,128)(2,1)} %copy.16), channel_id=1, source_target_pairs={{0,2},{1,3},{2,0},{3,1},{4,6},{5,7},{6,4},{7,5},{8,10},{9,11},{10,... | collective-permute-start | bytes 2162696 | tf_op jit(solution)/shard_map/ppermute | solution.py:34
  50.3 65.5 %collective-permute-start.4 = (bf16[512,704]{0,1:T(8,128)(2,1)}, bf16[512,704]{0,1:T(8,128)(2,1)}, u32[]{:S(2)}, u32[]{:S(2)}) collective-permute-start(bf16[512,704]{0,1:T(8,128)(2,1)} %copy.22), channel_id=1, source_target_pairs={{0,2},{1,3},{2,0},{3,1},{4,6},{5,7},{6,4},{7,5},{8,10},{9,11},{10,... | collective-permute-start | bytes 2162696 | tf_op jit(solution)/shard_map/ppermute | solution.py:34
  51.8 73.3 %collective-permute-start.2 = (bf16[512,704]{0,1:T(8,128)(2,1)}, bf16[512,704]{0,1:T(8,128)(2,1)}, u32[]{:S(2)}, u32[]{:S(2)}) collective-permute-start(bf16[512,704]{0,1:T(8,128)(2,1)} %copy.16), channel_id=1, source_target_pairs={{0,3},{1,2},{2,1},{3,0},{4,7},{5,6},{6,5},{7,4},{8,11},{9,10},{10,... | collective-permute-start | bytes 2162696 | tf_op jit(solution)/shard_map/ppermute | solution.py:34
  65.8 68.6 %collective-permute-start.5 = (bf16[512,704]{0,1:T(8,128)(2,1)}, bf16[512,704]{0,1:T(8,128)(2,1)}, u32[]{:S(2)}, u32[]{:S(2)}) collective-permute-start(bf16[512,704]{0,1:T(8,128)(2,1)} %copy.22), channel_id=1, source_target_pairs={{0,3},{1,2},{2,1},{3,0},{4,7},{5,6},{6,5},{7,4},{8,11},{9,10},{10,... | collective-permute-start | bytes 2162696 | tf_op jit(solution)/shard_map/ppermute | solution.py:34
  190.2 13.0 %collective-permute-start.6 = (bf16[4,352,2816]{2,1,0:T(8,128)(2,1)}, bf16[4,352,2816]{2,1,0:T(8,128)(2,1)}, u32[]{:S(2)}, u32[]{:S(2)}) collective-permute-start(bf16[4,352,2816]{2,1,0:T(8,128)(2,1)} %dynamic-slice_bitcast_fusion), channel_id=1, source_target_pairs={{0,4},{4,0},{8,12},{12,8},{16,20},{20,16},{24,28},{28,24},{1,5},{5... | collective-permute-start | bytes 23789576 | tf_op jit(solution)/shard_map/ppermute | solution.py:63
  213.8 87.4 %collective-permute-start.7 = (bf16[352,2816]{1,0:T(8,128)(2,1)}, bf16[352,2816]{1,0:T(8,128)(2,1)S(1)}, u32[]{:S(2)}, u32[]{:S(2)}) collective-permute-start(bf16[352,2816]{1,0:T(8,128)(2,1)} %get-tuple-element.138), channel_id=1, source_target_pairs={{0,8},{4,12},{1,9},{5,13},{2,10},{6,14},{3,11},{7,15}} | collective-permute-start | bytes 5947400 | tf_op jit(solution)/shard_map/ppermute | solution.py:73
  215.2 86.0 %collective-permute-start.9 = (bf16[352,2816]{1,0:T(8,128)(2,1)}, bf16[352,2816]{1,0:T(8,128)(2,1)}, u32[]{:S(2)}, u32[]{:S(2)}) collective-permute-start(bf16[352,2816]{1,0:T(8,128)(2,1)} %get-tuple-element.137), channel_id=1, source_target_pairs={{28,20},{24,16},{29,21},{25,17},{30,22},{26,18},{31,23},{27,19}} | collective-permute-start | bytes 5947400 | tf_op jit(solution)/shard_map/ppermute | solution.py:74
  306.4 53.2 %collective-permute-start.10 = (bf16[352,2816]{1,0:T(8,128)(2,1)}, bf16[352,2816]{1,0:T(8,128)(2,1)S(1)}, u32[]{:S(2)}, u32[]{:S(2)}) collective-permute-start(bf16[352,2816]{1,0:T(8,128)(2,1)} %get-tuple-element.135), channel_id=1, source_target_pairs={{28,20},{24,16},{20,12},{16,8},{29,21},{25,17},{21,13},{17,9},{30,... | collective-permute-start | bytes 5947400 | tf_op jit(solution)/shard_map/ppermute | solution.py:74
  307.2 71.3 %collective-permute-start.8 = (bf16[352,2816]{1,0:T(8,128)(2,1)}, bf16[352,2816]{1,0:T(8,128)(2,1)}, u32[]{:S(2)}, u32[]{:S(2)}) collective-permute-start(bf16[352,2816]{1,0:T(8,128)(2,1)} %get-tuple-element.136), channel_id=1, source_target_pairs={{0,8},{4,12},{8,16},{12,20},{1,9},{5,13},{9,17},{13,21},{2,10},{6,... | collective-permute-start | bytes 5947400 | tf_op jit(solution)/shard_map/ppermute | solution.py:73
  425.7 29.2 %collective-permute-start.14 = (bf16[512,704]{0,1:T(8,128)(2,1)}, bf16[512,704]{0,1:T(8,128)(2,1)}, u32[]{:S(2)}, u32[]{:S(2)}) collective-permute-start(bf16[512,704]{0,1:T(8,128)(2,1)} %copy.34), channel_id=1, source_target_pairs={{0,1},{1,0},{2,3},{3,2},{4,5},{5,4},{6,7},{7,6},{8,9},{9,8},{10,11... | collective-permute-start | bytes 2162696 | tf_op jit(solution)/shard_map/ppermute | solution.py:47
  428.6 34.5 %collective-permute-start.15 = (bf16[512,704]{0,1:T(8,128)(2,1)}, bf16[512,704]{0,1:T(8,128)(2,1)}, u32[]{:S(2)}, u32[]{:S(2)}) collective-permute-start(bf16[512,704]{0,1:T(8,128)(2,1)} %copy.36), channel_id=1, source_target_pairs={{0,2},{1,3},{2,0},{3,1},{4,6},{5,7},{6,4},{7,5},{8,10},{9,11},{10,... | collective-permute-start | bytes 2162696 | tf_op jit(solution)/shard_map/ppermute | solution.py:47
  431.2 34.2 %collective-permute-start.16 = (bf16[512,704]{0,1:T(8,128)(2,1)}, bf16[512,704]{0,1:T(8,128)(2,1)}, u32[]{:S(2)}, u32[]{:S(2)}) collective-permute-start(bf16[512,704]{0,1:T(8,128)(2,1)} %copy.38), channel_id=1, source_target_pairs={{0,3},{1,2},{2,1},{3,0},{4,7},{5,6},{6,5},{7,4},{8,11},{9,10},{10,... | collective-permute-start | bytes 2162696 | tf_op jit(solution)/shard_map/ppermute | solution.py:47
  449.6 26.5 %collective-permute-start.11 = (bf16[512,704]{0,1:T(8,128)(2,1)}, bf16[512,704]{0,1:T(8,128)(2,1)}, u32[]{:S(2)}, u32[]{:S(2)}) collective-permute-start(bf16[512,704]{0,1:T(8,128)(2,1)} %copy.28), channel_id=1, source_target_pairs={{0,1},{1,0},{2,3},{3,2},{4,5},{5,4},{6,7},{7,6},{8,9},{9,8},{10,11... | collective-permute-start | bytes 2162696 | tf_op jit(solution)/shard_map/ppermute | solution.py:47
  452.4 40.3 %collective-permute-start.12 = (bf16[512,704]{0,1:T(8,128)(2,1)}, bf16[512,704]{0,1:T(8,128)(2,1)S(1)}, u32[]{:S(2)}, u32[]{:S(2)}) collective-permute-start(bf16[512,704]{0,1:T(8,128)(2,1)} %copy.30), channel_id=1, source_target_pairs={{0,2},{1,3},{2,0},{3,1},{4,6},{5,7},{6,4},{7,5},{8,10},{9,11},{10,... | collective-permute-start | bytes 2162696 | tf_op jit(solution)/shard_map/ppermute | solution.py:47
  455.0 38.8 %collective-permute-start.13 = (bf16[512,704]{0,1:T(8,128)(2,1)}, bf16[512,704]{0,1:T(8,128)(2,1)S(1)}, u32[]{:S(2)}, u32[]{:S(2)}) collective-permute-start(bf16[512,704]{0,1:T(8,128)(2,1)} %copy.32), channel_id=1, source_target_pairs={{0,3},{1,2},{2,1},{3,0},{4,7},{5,6},{6,5},{7,4},{8,11},{9,10},{10,... | collective-permute-start | bytes 2162696 | tf_op jit(solution)/shard_map/ppermute | solution.py:47
  524.4 91.3 %copy-start.22 = (f32[704]{0:T(1024)S(1)}, f32[704]{0:T(1024)}, u32[]{:S(2)}) copy-start(f32[704]{0:T(1024)} %copy-done.21) | copy-start | bytes 8452
  524.4 91.3 %copy-start.24 = (f32[704]{0:T(1024)S(1)}, f32[704]{0:T(1024)}, u32[]{:S(2)}) copy-start(f32[704]{0:T(1024)} %copy-done.23) | copy-start | bytes 8452
  524.4 91.2 %copy-start.26 = (f32[704]{0:T(1024)S(1)}, f32[704]{0:T(1024)}, u32[]{:S(2)}) copy-start(f32[704]{0:T(1024)} %copy-done.25) | copy-start | bytes 8452
  524.4 91.2 %copy-start.28 = (f32[704]{0:T(1024)S(1)}, f32[704]{0:T(1024)}, u32[]{:S(2)}) copy-start(f32[704]{0:T(1024)} %copy-done.27) | copy-start | bytes 8452
  524.4 91.2 %copy-start.30 = (f32[704]{0:T(1024)S(1)}, f32[704]{0:T(1024)}, u32[]{:S(2)}) copy-start(f32[704]{0:T(1024)} %copy-done.29) | copy-start | bytes 8452
  524.4 91.2 %copy-start.32 = (f32[704]{0:T(1024)S(1)}, f32[704]{0:T(1024)}, u32[]{:S(2)}) copy-start(f32[704]{0:T(1024)} %copy-done.31) | copy-start | bytes 8452
  524.5 91.2 %copy-start.34 = (f32[704]{0:T(1024)S(1)}, f32[704]{0:T(1024)}, u32[]{:S(2)}) copy-start(f32[704]{0:T(1024)} %copy-done.33) | copy-start | bytes 8452
  524.5 91.2 %copy-start.36 = (f32[704]{0:T(1024)S(1)}, f32[704]{0:T(1024)}, u32[]{:S(2)}) copy-start(f32[704]{0:T(1024)} %copy-done.35) | copy-start | bytes 8452
  524.5 91.2 %copy-start.38 = (f32[704]{0:T(1024)S(1)}, f32[704]{0:T(1024)}, u32[]{:S(2)}) copy-start(f32[704]{0:T(1024)} %copy-done.37) | copy-start | bytes 8452
  524.5 91.2 %copy-start.40 = (f32[704]{0:T(1024)S(1)}, f32[704]{0:T(1024)}, u32[]{:S(2)}) copy-start(f32[704]{0:T(1024)} %copy-done.39) | copy-start | bytes 8452
  524.5 91.2 %copy-start.42 = (f32[704]{0:T(1024)S(1)}, f32[704]{0:T(1024)}, u32[]{:S(2)}) copy-start(f32[704]{0:T(1024)} %copy-done.41) | copy-start | bytes 8452
  524.5 91.2 %copy-start.44 = (f32[704]{0:T(1024)S(1)}, f32[704]{0:T(1024)}, u32[]{:S(2)}) copy-start(f32[704]{0:T(1024)} %copy-done.43) | copy-start | bytes 8452
  524.5 91.2 %copy-start.46 = (f32[704]{0:T(1024)S(1)}, f32[704]{0:T(1024)}, u32[]{:S(2)}) copy-start(f32[704]{0:T(1024)} %copy-done.45) | copy-start | bytes 8452
  524.5 91.2 %copy-start.48 = (f32[704]{0:T(1024)S(1)}, f32[704]{0:T(1024)}, u32[]{:S(2)}) copy-start(f32[704]{0:T(1024)} %copy-done.47) | copy-start | bytes 8452
  524.5 91.2 %copy-start.50 = (f32[704]{0:T(1024)S(1)}, f32[704]{0:T(1024)}, u32[]{:S(2)}) copy-start(f32[704]{0:T(1024)} %copy-done.49) | copy-start | bytes 8452
  524.5 91.2 %copy-start.52 = (f32[704]{0:T(1024)S(1)}, f32[704]{0:T(1024)}, u32[]{:S(2)}) copy-start(f32[704]{0:T(1024)} %copy-done.51) | copy-start | bytes 8452
  524.6 91.2 %copy-start.54 = (f32[704]{0:T(1024)S(1)}, f32[704]{0:T(1024)}, u32[]{:S(2)}) copy-start(f32[704]{0:T(1024)} %copy-done.53) | copy-start | bytes 8452
  524.6 91.2 %copy-start.56 = (f32[704]{0:T(1024)S(1)}, f32[704]{0:T(1024)}, u32[]{:S(2)}) copy-start(f32[704]{0:T(1024)} %copy-done.55) | copy-start | bytes 8452
  524.6 91.2 %copy-start.58 = (f32[704]{0:T(1024)S(1)}, f32[704]{0:T(1024)}, u32[]{:S(2)}) copy-start(f32[704]{0:T(1024)} %copy-done.57) | copy-start | bytes 8452
  524.6 91.2 %copy-start.60 = (f32[704]{0:T(1024)S(1)}, f32[704]{0:T(1024)}, u32[]{:S(2)}) copy-start(f32[704]{0:T(1024)} %copy-done.59) | copy-start | bytes 8452
  524.6 91.2 %copy-start.62 = (f32[704]{0:T(1024)S(1)}, f32[704]{0:T(1024)}, u32[]{:S(2)}) copy-start(f32[704]{0:T(1024)} %copy-done.61) | copy-start | bytes 8452
  524.6 91.2 %copy-start.64 = (f32[704]{0:T(1024)S(1)}, f32[704]{0:T(1024)}, u32[]{:S(2)}) copy-start(f32[704]{0:T(1024)} %copy-done.63) | copy-start | bytes 8452
  524.6 91.2 %copy-start.66 = (f32[704]{0:T(1024)S(1)}, f32[704]{0:T(1024)}, u32[]{:S(2)}) copy-start(f32[704]{0:T(1024)} %copy-done.65) | copy-start | bytes 8452
  524.6 91.2 %copy-start.68 = (f32[704]{0:T(1024)S(1)}, f32[704]{0:T(1024)}, u32[]{:S(2)}) copy-start(f32[704]{0:T(1024)} %copy-done.67) | copy-start | bytes 8452
  524.6 91.2 %copy-start.70 = (f32[704]{0:T(1024)S(1)}, f32[704]{0:T(1024)}, u32[]{:S(2)}) copy-start(f32[704]{0:T(1024)} %copy-done.69) | copy-start | bytes 8452
  524.6 91.2 %copy-start.72 = (f32[704]{0:T(1024)S(1)}, f32[704]{0:T(1024)}, u32[]{:S(2)}) copy-start(f32[704]{0:T(1024)} %copy-done.71) | copy-start | bytes 8452
  524.7 91.2 %copy-start.74 = (f32[704]{0:T(1024)S(1)}, f32[704]{0:T(1024)}, u32[]{:S(2)}) copy-start(f32[704]{0:T(1024)} %copy-done.73) | copy-start | bytes 8452
  524.7 91.2 %copy-start.76 = (f32[704]{0:T(1024)S(1)}, f32[704]{0:T(1024)}, u32[]{:S(2)}) copy-start(f32[704]{0:T(1024)} %copy-done.75) | copy-start | bytes 8452
  524.7 91.2 %copy-start.78 = (f32[704]{0:T(1024)S(1)}, f32[704]{0:T(1024)}, u32[]{:S(2)}) copy-start(f32[704]{0:T(1024)} %copy-done.77) | copy-start | bytes 8452
  524.7 91.2 %copy-start.80 = (f32[704]{0:T(1024)S(1)}, f32[704]{0:T(1024)}, u32[]{:S(2)}) copy-start(f32[704]{0:T(1024)} %copy-done.79) | copy-start | bytes 8452
  524.7 91.2 %copy-start.82 = (f32[704]{0:T(1024)S(1)}, f32[704]{0:T(1024)}, u32[]{:S(2)}) copy-start(f32[704]{0:T(1024)} %copy-done.81) | copy-start | bytes 8452
  524.7 91.2 %copy-start.84 = (f32[704]{0:T(1024)S(1)}, f32[704]{0:T(1024)}, u32[]{:S(2)}) copy-start(f32[704]{0:T(1024)} %copy-done.83) | copy-start | bytes 8452
  524.7 91.2 %copy-start.86 = (f32[704]{0:T(1024)S(1)}, f32[704]{0:T(1024)}, u32[]{:S(2)}) copy-start(f32[704]{0:T(1024)} %copy-done.85) | copy-start | bytes 8452
  524.7 91.2 %copy-start.88 = (f32[704]{0:T(1024)S(1)}, f32[704]{0:T(1024)}, u32[]{:S(2)}) copy-start(f32[704]{0:T(1024)} %copy-done.87) | copy-start | bytes 8452
  524.7 91.2 %copy-start.90 = (f32[704]{0:T(1024)S(1)}, f32[704]{0:T(1024)}, u32[]{:S(2)}) copy-start(f32[704]{0:T(1024)} %copy-done.89) | copy-start | bytes 8452
  524.7 91.2 %copy-start.92 = (f32[704]{0:T(1024)S(1)}, f32[704]{0:T(1024)}, u32[]{:S(2)}) copy-start(f32[704]{0:T(1024)} %copy-done.91) | copy-start | bytes 8452
  524.8 91.2 %copy-start.94 = (f32[704]{0:T(1024)S(1)}, f32[704]{0:T(1024)}, u32[]{:S(2)}) copy-start(f32[704]{0:T(1024)} %copy-done.93) | copy-start | bytes 8452
  524.8 91.2 %copy-start.96 = (f32[704]{0:T(1024)S(1)}, f32[704]{0:T(1024)}, u32[]{:S(2)}) copy-start(f32[704]{0:T(1024)} %copy-done.95) | copy-start | bytes 8452
  524.8 12.8 %collective-permute-start.17 = (f32[52,704]{1,0:T(8,128)S(1)}, f32[52,704]{1,0:T(8,128)S(1)}, u32[]{:S(2)}, u32[]{:S(2)}) collective-permute-start(f32[52,704]{1,0:T(8,128)S(1)} %pad_maximum_fusion), channel_id=1, source_target_pairs={{0,4},{4,0},{8,12},{12,8},{16,20},{20,16},{24,28},{28,24},{1,5},{5... | collective-permute-start | bytes 439304 | tf_op jit(solution)/shard_map/ppermute | solution.py:85
  524.9 91.2 %copy-start.4 = (f32[512,704]{1,0:T(8,128)S(1)}, f32[512,704]{1,0:T(8,128)}, u32[]{:S(2)}) copy-start(f32[512,704]{1,0:T(8,128)} %copy-done.3) | copy-start | bytes 4325380
  530.7 100.0 %collective-permute-start.20 = (bf16[352,2816]{1,0:T(8,128)(2,1)}, bf16[352,2816]{1,0:T(8,128)(2,1)}, u32[]{:S(2)}, u32[]{:S(2)}) collective-permute-start(bf16[352,2816]{1,0:T(8,128)(2,1)} %get-tuple-element.133), channel_id=1, source_target_pairs={{0,8},{4,12},{8,16},{12,20},{16,24},{20,28},{1,9},{5,13},{9,17},{1... | collective-permute-start | bytes 5947400 | tf_op jit(solution)/shard_map/ppermute | solution.py:73
  536.2 94.4 %collective-permute-start.21 = (bf16[352,2816]{1,0:T(8,128)(2,1)}, bf16[352,2816]{1,0:T(8,128)(2,1)}, u32[]{:S(2)}, u32[]{:S(2)}) collective-permute-start(bf16[352,2816]{1,0:T(8,128)(2,1)} %get-tuple-element.134), channel_id=1, source_target_pairs={{28,20},{24,16},{20,12},{16,8},{12,4},{8,0},{29,21},{25,17},{21,13... | collective-permute-start | bytes 5947400 | tf_op jit(solution)/shard_map/ppermute | solution.py:74
  537.6 76.0 %collective-permute-start.18 = (f32[52,704]{1,0:T(8,128)S(1)}, f32[52,704]{1,0:T(8,128)S(1)}, u32[]{:S(2)}, u32[]{:S(2)}) collective-permute-start(f32[52,704]{1,0:T(8,128)S(1)} %fusion.123), channel_id=1, source_target_pairs={{0,8},{4,12},{8,0},{12,4},{16,24},{20,28},{24,16},{28,20},{1,9},{5... | collective-permute-start | bytes 439304 | tf_op jit(solution)/shard_map/ppermute | solution.py:85
  613.6 15.7 %collective-permute-start.19 = (f32[52,704]{1,0:T(8,128)S(1)}, f32[52,704]{1,0:T(8,128)S(1)}, u32[]{:S(2)}, u32[]{:S(2)}) collective-permute-start(f32[52,704]{1,0:T(8,128)S(1)} %add.568), channel_id=1, source_target_pairs={{0,16},{4,20},{8,24},{12,28},{16,0},{20,4},{24,8},{28,12},{1,17},{... | collective-permute-start | bytes 439304 | tf_op jit(solution)/shard_map/ppermute | solution.py:85
  (65 other events, 884.5 us)
Sparse Core Ops, SparseCore 0:
  9.7 146.2 all-gather.2
  157.6 201.9 all-gather.4
  407.5 188.7 reduce-scatter.1
where the time goes:
time: 652 us; the launch traced here: 646 us
  waiting for transfers between devices  289 us (44%)
  local copies, waits for them, and re-layouts  121 us (19%)
  matrix products  81.9 us (13%)
  other arithmetic  72.9 us (11%)
  starting transfers between devices  36.4 us (6%)
  blocking collectives  28.9 us (4%)
  between operations  16 us (2%)
    ppermute x3, waiting for transfers between devices, dp_line_scatter(): up = lax.ppermute(high, 'dp', [(i, i + 2) for i in senders])  103 us
    ppermute x3, waiting for transfers between devices, dp_total(): value = value + lax.ppermute(value, 'dp', swap_pairs(shift, n))  73.3 us
    dynamic_update_slice x8, local copies, waits for them, and re-layouts, chan_gather(): whole = lax.dynamic_update_slice(whole, parts[k], (0, (me ^ k) * width))  64.5 us
    all_gather x1, waiting for transfers between devices, body(): reduce_all = lax.all_gather(w_reduce, 'dp', axis=1, tiled=True)  46.3 us
    ppermute x6, waiting for transfers between devices, chan_scatter(): lax.ppermute(mine, 'chan', swap_pairs(k, n)).astype(jnp.float32)  28.1 us
    dot_general x1, matrix products, body(): lax.dot_general(dbranch_all, reduce_all, (((1,), (1,)), ((), ())), prefer...  15.5 us
    dot_general x1, matrix products, body(): pre = jnp.dot(normed_all, expand_all, preferred_element_type=jnp.float32)  15.2 us
    dot_general x1, matrix products, body(): lax.dot_general(dpre, expand_all, (((1,), (1,)), ((), ())), preferred_ele...  13.8 us
  transfers between devices with their start and end apart: 25, of which 10 were waited for; matrix products, arithmetic and copies ran while one was open for 37% of the time, Pallas kernels for 0%

commit v1 on v0

--- a/solution.py
+++ b/solution.py
@@ -5,6 +5,18 @@
 from jax.sharding import PartitionSpec as P
 
 eps = 1e-06
+
+
+def gather_by_bits(shard, axis, dim):
+    ways, here = (lax.axis_size(axis), lax.axis_index(axis))
+    grown, reach = (shard, 1)
+    while reach < ways:
+        theirs = lax.ppermute(grown, axis, [(d, d ^ reach) for d in range(ways)])
+        mine_first = jnp.concatenate([grown, theirs], axis=dim)
+        theirs_first = jnp.concatenate([theirs, grown], axis=dim)
+        grown = jnp.where(here & reach == 0, mine_first, theirs_first)
+        reach = 2 * reach
+    return grown
 
 
 def depthwise(field, kern):
@@ -114,7 +126,7 @@
     reduce_part = lax.dot_general(
         dbranch_all, hidden, (((0,), (0,)), ((), ())), preferred_element_type=jnp.float32
     ).astype(jnp.bfloat16)
-    reduce_all = lax.all_gather(w_reduce, "dp", axis=1, tiled=True)
+    reduce_all = gather_by_bits(w_reduce, "dp", 1)
     grad_reduce, reduce_all = dp_line_scatter(reduce_part, reduce_all)
     grad_reduce = grad_reduce.T
     dhidden = lax.dot_general(

time: 652 us -> 897 us (1.38)
  waiting for transfers between devices: 289 us -> 481 us
  other arithmetic: 72.9 us -> 103 us
  starting transfers between devices: 36.4 us -> 64.2 us
    ppermute x0 -> x3, waiting for transfers between devices: none -> 161 us  [gather_by_bits(): theirs = lax.ppermute(grown, axis, [(d, d ^ reach) for d in range(ways)])]
    ppermute x3, waiting for transfers between devices: 103 us -> 187 us  [dp_line_scatter(): up = lax.ppermute(high, 'dp', [(i, i + 2) for i in senders])]
    all_gather x1 -> x0, waiting for transfers between devices: 46.3 us -> none  [body(): reduce_all = lax.all_gather(w_reduce, 'dp', axis=1, tiled=True)]
    select_n x0 -> x3, other arithmetic: none -> 29.6 us  [gather_by_bits(): grown = jnp.where(here & reach == 0, mine_first, theirs_first)]
    ppermute x3, starting transfers between devices: 13 us -> 36.7 us  [dp_line_scatter(): up = lax.ppermute(high, 'dp', [(i, i + 2) for i in senders])]
    ppermute x6, waiting for transfers between devices: 12.6 us -> 28.7 us  [chan_gather(): lax.ppermute(block, 'chan', swap_pairs(k, n))]
    ppermute x1, waiting for transfers between devices: 12.7 us -> 0.01 us  [dp_line_scatter(): own = own + lax.ppermute(other, 'dp', swap_pairs(1, n))]
    all_gather x1, waiting for transfers between devices: 12.2 us -> 0.01 us  [body(): expand_all = lax.all_gather(w_expand, 'dp', axis=0, tiled=True)]
  transfers between devices with their start and end apart: 25 -> 27, of which waited for: 10 -> 9; matrix products, arithmetic and copies ran while one was open for 37% -> 29% of each run, Pallas kernels for 0% -> 0%
where the time goes in v1:
time: 897 us; the launch traced here: 891 us
  waiting for transfers between devices  481 us (54%)
  local copies, waits for them, and re-layouts  118 us (13%)
  other arithmetic  103 us (11%)
  matrix products  80.1 us (9%)
  starting transfers between devices  64.2 us (7%)
  blocking collectives  29.1 us (3%)
  between operations  16.3 us (2%)
    ppermute x3, waiting for transfers between devices, dp_line_scatter(): up = lax.ppermute(high, 'dp', [(i, i + 2) for i in senders])  187 us
    ppermute x3, waiting for transfers between devices, gather_by_bits(): theirs = lax.ppermute(grown, axis, [(d, d ^ reach) for d in range(ways)])  161 us
    ppermute x3, waiting for transfers between devices, dp_total(): value = value + lax.ppermute(value, 'dp', swap_pairs(shift, n))  74.7 us
    dynamic_update_slice x8, local copies, waits for them, and re-layouts, chan_gather(): whole = lax.dynamic_update_slice(whole, parts[k], (0, (me ^ k) * width))  64.5 us
    ppermute x3, starting transfers between devices, dp_line_scatter(): up = lax.ppermute(high, 'dp', [(i, i + 2) for i in senders])  36.7 us
    select_n x3, other arithmetic, gather_by_bits(): grown = jnp.where(here & reach == 0, mine_first, theirs_first)  29.6 us
    ppermute x6, waiting for transfers between devices, chan_gather(): lax.ppermute(block, 'chan', swap_pairs(k, n))  28.7 us
    ppermute x6, waiting for transfers between devices, chan_scatter(): lax.ppermute(mine, 'chan', swap_pairs(k, n)).astype(jnp.float32)  28.1 us
  transfers between devices with their start and end apart: 27, of which 9 were waited for; matrix products, arithmetic and copies ran while one was open for 29% of the time, Pallas kernels for 0%

profile of v1, /device:TPU:0, one launch (start us, length us, event | category | flops | bytes accessed | tf_op | source)
XLA Modules:
  0.0 891.4 jit_solution(18271927032694524080)
XLA Ops:
  10.3 13.0 %fusion.110 = (f32[2,16,16]{2,1,0:T(8,128)S(1)}, f32[2,16,16,704]{3,2,1,0:T(8,128)S(1)}) fusion(f32[704]{0:T(1024)S(1)} %get-tuple-element.125, f32[704]{0:T(1024)S(1)} %get-tuple-element.126, f32[704]{0:T(1024)S(1)} %get-tuple-element.79, f32[704]{0:T(1024)S(1)} %get-tuple-element.80, f32[704]{0:T(1024)S(1)} %get-tuple-element.81, ...), kind=kLoop, calls=%fused_computation.357 | loop fusion | flops 35323392 | bytes 3023616 | tf_op jit(solution)/shard_map/reduce_sum | solution.py:113
  23.7 11.3 %psum.28 = f32[512]{0:T(512)S(1)} all-reduce(f32[512]{0:T(512)S(1)} %reduce_sum.509), channel_id=1, replica_groups=mesh['dp'=8,'chan'=4] {'chan'}, use_global_device_ids=true, to_apply=%region_1.2 | all-reduce | flops 512 | bytes 4096 | tf_op jit(solution)/shard_map/psum | solution.py:113
  35.5 8.5 psum.29
  45.6 1.5 collective-permute-start
  48.7 1.4 collective-permute-start.4
  50.2 14.8 %collective-permute-done = bf16[512,704]{0,1:T(8,128)(2,1)} collective-permute-done((bf16[512,704]{0,1:T(8,128)(2,1)}, bf16[512,704]{0,1:T(8,128)(2,1)}, u32[]{:S(2)}, u32[]{:S(2)}) %collective-permute-start) | collective-permute-done | bytes 720928 | tf_op jit(solution)/shard_map/ppermute | solution.py:46
  65.0 1.5 collective-permute-start.2
  66.5 13.8 %collective-permute-done.3 = bf16[512,704]{0,1:T(8,128)(2,1)S(1)} collective-permute-done((bf16[512,704]{0,1:T(8,128)(2,1)S(1)}, bf16[512,704]{0,1:T(8,128)(2,1)S(1)}, u32[]{:S(2)}, u32[]{:S(2)}) %collective-permute-start.3) | collective-permute-done | bytes 720928 | tf_op jit(solution)/shard_map/ppermute | solution.py:46
  80.3 1.5 collective-permute-start.5
  81.9 1.8 broadcast.41.clone
  83.6 7.8 dynamic_update_slice.24
  91.4 1.7 broadcast.41.clone.1
  93.2 7.9 dynamic_update_slice.28
  101.1 1.4 copy.17
  102.5 8.7 dynamic_update_slice.25
  111.4 8.7 dynamic_update_slice.29
  121.5 7.7 dynamic_update_slice.26
  130.7 7.8 dynamic_update_slice.30
  139.9 8.0 dynamic_update_slice.27
  147.8 1.5 copy.27
  149.4 8.0 dynamic_update_slice.31
  157.4 4.0 maximum_select_fusion.2
  161.3 1.6 collective-permute-start.12
  162.9 15.1 %multiply_convert_fusion = (bf16[512,2816]{1,0:T(8,128)(2,1)S(1)}, f32[512,2816]{1,0:T(8,128)}) fusion(bf16[512,2816]{1,0:T(8,128)(2,1)} %dynamic_update_slice.27, bf16[2816,2816]{1,0:T(8,128)(2,1)} %all-gather.2.cloned.1.call-done), kind=kOutput, calls=%fused_computation.109 | convolution fusion | flops 8127381504 | bytes 27394048 | tf_op jit(solution)/shard_map/dot_general | solution.py:121
  178.0 12.1 %convolution_convert_fusion.1 = bf16[2816,2816]{1,0:T(8,128)(2,1)} fusion(bf16[512,2816]{1,0:T(8,128)(2,1)S(1)} %copy-done.16, bf16[512,2816]{1,0:T(8,128)(2,1)S(1)} %get-tuple-element.16), kind=kOutput, calls=%fused_computation.97 | convolution fusion | flops 8128102400 | bytes 21626880 | tf_op jit(solution)/shard_map/dot_general | solution.py:126
  190.1 6.8 dynamic-slice_bitcast_fusion
  196.9 45.1 %collective-permute-done.12 = bf16[2816,704]{0,1:T(8,128)(2,1)} collective-permute-done((bf16[2816,704]{0,1:T(8,128)(2,1)}, bf16[2816,704]{0,1:T(8,128)(2,1)}, u32[]{:S(2)}, u32[]{:S(2)}) %collective-permute-start.12) | collective-permute-done | bytes 3964960 | tf_op jit(solution)/shard_map/ppermute | solution.py:14
  242.0 10.1 %maximum_select_fusion.1 = bf16[2816,1408]{0,1:T(8,128)(2,1)} fusion(bf16[2816,704]{0,1:T(8,128)(2,1)} %collective-permute-done.12, bf16[2816,704]{0,1:T(8,128)(2,1)} %maximum_select_fusion.2, pred[]{:T(512)S(6)} %eq.12), kind=kLoop, calls=%fused_computation.100 | loop fusion | flops 35684352 | bytes 15859713 | tf_op jit(solution)/shard_map/jit(_where)/select_n | solution.py:17
  252.1 2.4 collective-permute-start.13
  254.5 6.1 bitcast_add_fusion
  260.6 2.3 dynamic-slice_bitcast_fusion.1
  263.0 2.0 copy-done
  265.0 2.0 collective-permute-start.9
  267.0 5.0 collective-permute-start.7
  272.0 187.1 %collective-permute-done.7 = bf16[352,2816]{1,0:T(8,128)(2,1)} collective-permute-done((bf16[352,2816]{1,0:T(8,128)(2,1)}, bf16[352,2816]{1,0:T(8,128)(2,1)}, u32[]{:S(2)}, u32[]{:S(2)}) %collective-permute-start.7) | collective-permute-done | bytes 1982496 | tf_op jit(solution)/shard_map/ppermute | solution.py:85
  459.1 5.7 bitcast_add_fusion.3
  464.7 5.6 collective-permute-start.8
  470.4 2.0 collective-permute-start.10
  472.4 116.4 %collective-permute-done.13 = bf16[2816,1408]{0,1:T(8,128)(2,1)} collective-permute-done((bf16[2816,1408]{0,1:T(8,128)(2,1)}, bf16[2816,1408]{0,1:T(8,128)(2,1)}, u32[]{:S(2)}, u32[]{:S(2)}) %collective-permute-start.13) | collective-permute-done | bytes 7929888 | tf_op jit(solution)/shard_map/ppermute | solution.py:14
  588.8 15.6 %maximum_select_fusion = bf16[2816,2816]{0,1:T(8,128)(2,1)S(1)} fusion(bf16[2816,1408]{0,1:T(8,128)(2,1)} %collective-permute-done.13, bf16[2816,1408]{0,1:T(8,128)(2,1)} %maximum_select_fusion.1, pred[]{:T(512)S(6)} %eq.11), kind=kLoop, calls=%fused_computation.98 | loop fusion | flops 71368704 | bytes 31719424 | tf_op jit(solution)/shard_map/jit(_where)/select_n | solution.py:17
  604.4 5.5 copy-done.7
  609.9 12.1 %fusion.5 = bf16[512,2816]{1,0:T(8,128)(2,1)} fusion(f32[512,2816]{1,0:T(8,128)} %get-tuple-element.148, bf16[512,2816]{1,0:T(8,128)(2,1)S(1)} %copy-done.16, bf16[2816,2816]{0,1:T(8,128)(2,1)S(1)} %maximum_select_fusion), kind=kOutput, calls=%fused_computation.108 | convolution fusion | flops 8134590464 | bytes 27394048 | tf_op jit(solution)/shard_map/dot_general | solution.py:132
  622.0 13.7 %convolution_convert_fusion = bf16[2816,2816]{1,0:T(8,128)(2,1)} fusion(bf16[512,2816]{1,0:T(8,128)(2,1)S(1)} %copy-done.17, bf16[512,2816]{1,0:T(8,128)(2,1)} %fusion.5), kind=kOutput, calls=%fused_computation.96 | convolution fusion | flops 8128102400 | bytes 21626880 | tf_op jit(solution)/shard_map/dot_general | solution.py:137
  635.7 1.8 copy-done.107
  637.5 13.0 %convolution_convert_fusion.3 = bf16[512,2816]{1,0:T(8,128)(2,1)S(1)} fusion(bf16[512,2816]{1,0:T(8,128)(2,1)S(1)} %copy-done.107, bf16[2816,2816]{0,1:T(8,128)(2,1)} %copy-done.7), kind=kOutput, calls=%fused_computation.112 | convolution fusion | flops 8121614336 | bytes 21626880 | tf_op jit(solution)/shard_map/dot_general | solution.py:148
  658.9 14.1 %convolution_convert_fusion.2 = bf16[512,2816]{1,0:T(8,128)(2,1)S(1)} fusion(bf16[512,2816]{1,0:T(8,128)(2,1)} %fusion.5, bf16[2816,2816]{1,0:T(8,128)(2,1)} %all-gather.2.cloned.1.call-done), kind=kOutput, calls=%fused_computation.111 | convolution fusion | flops 8121614336 | bytes 21626880 | tf_op jit(solution)/shard_map/dot_general | solution.py:144
  682.7 6.3 collective-permute-done.15
  689.0 2.3 copy.31
  691.3 2.3 copy.29
  693.5 10.8 %collective-permute-done.19 = bf16[512,704]{0,1:T(8,128)(2,1)S(1)} collective-permute-done((bf16[512,704]{0,1:T(8,128)(2,1)}, bf16[512,704]{0,1:T(8,128)(2,1)S(1)}, u32[]{:S(2)}, u32[]{:S(2)}) %collective-permute-start.19) | collective-permute-done | bytes 720928 | tf_op jit(solution)/shard_map/ppermute | solution.py:59
  705.5 11.0 %collective-permute-done.18 = bf16[512,704]{0,1:T(8,128)(2,1)S(1)} collective-permute-done((bf16[512,704]{0,1:T(8,128)(2,1)}, bf16[512,704]{0,1:T(8,128)(2,1)S(1)}, u32[]{:S(2)}, u32[]{:S(2)}) %collective-permute-start.18) | collective-permute-done | bytes 720928 | tf_op jit(solution)/shard_map/ppermute | solution.py:59
  718.8 5.5 fusion.107
  724.4 9.3 %all-reduce.2 = (f32[512]{0:T(512)S(1)}, f32[512]{0:T(512)S(1)}) all-reduce(f32[512]{0:T(512)S(1)} %get-tuple-element.151, f32[512]{0:T(512)S(1)} %get-tuple-element.150), channel_id=1, replica_groups=mesh['dp'=8,'chan'=4] {'chan'}, use_global_device_ids=true, to_apply=%region_7.8 | all-reduce | flops 1024 | bytes 8192 | tf_op jit(solution)/shard_map/psum | solution.py:156
  733.7 6.6 multiply_reduce_fusion.2
  740.3 2.8 multiply_reduce_fusion.3
  743.2 4.1 multiply_reduce_fusion.1
  748.8 5.9 bitcast_add_fusion.2
  754.7 1.4 collective-permute-start.24
  756.1 26.1 %collective-permute-start.23 = (bf16[352,2816]{1,0:T(8,128)(2,1)}, bf16[352,2816]{1,0:T(8,128)(2,1)}, u32[]{:S(2)}, u32[]{:S(2)}) collective-permute-start(bf16[352,2816]{1,0:T(8,128)(2,1)} %get-tuple-element.133), channel_id=1, source_target_pairs={{0,8},{4,12},{8,16},{12,20},{16,24},{20,28},{1,9},{5,13},{9,17},{1... | collective-permute-start | bytes 5947400 | tf_op jit(solution)/shard_map/ppermute | solution.py:85
  783.5 74.7 %collective-permute-done.21 = f32[52,704]{1,0:T(8,128)S(1)} collective-permute-done((f32[52,704]{1,0:T(8,128)S(1)}, f32[52,704]{1,0:T(8,128)S(1)}, u32[]{:S(2)}, u32[]{:S(2)}) %collective-permute-start.21) | collective-permute-done | bytes 146464 | tf_op jit(solution)/shard_map/ppermute | solution.py:97
  858.2 2.1 collective-permute-start.22
  860.6 13.3 %fusion.101 = bf16[2,16,16,704]{3,2,1,0:T(8,128)(2,1)} fusion(f32[2,16,16,704]{3,2,1,0:T(8,128)S(1)} %bitcast.124, bf16[2,16,16,704]{3,2,1,0:T(8,128)(2,1)S(1)} %copy-done.9, f32[704]{0:T(1024)S(1)} %copy-done.46, f32[704]{0:T(1024)S(1)} %copy-done.48, f32[704]{0:T(1024)S(1)} %copy-done.52, f32[704]{0:T(1024)S(1)} %copy-done.54, f32[704]{0:T(1024)S(1)} %copy-done.56, ...), kind=kLoop, calls=%fused_computation.216 | loop fusion | flops 36044800 | bytes 3021568 | tf_op jit(solution)/shard_map/convert_element_type | solution.py:184
  875.3 5.3 fusion.7
  880.6 3.7 convert_element_type.100
  (352 shorter events, 36.1 us)
Async XLA Ops:
  7.2 155.7 %all-gather.2.cloned.1.call-start = ((), (), s32[]{:S(2)}) async-start(), calls=%async_computation.1 | async-start | bytes 17842176 | tf_op jit(solution)/shard_map/all_gather | solution.py:120
  7.9 872.7 %reduce-scatter.2.cloned.1.call-start = ((), (), s32[]{:S(2)}) async-start(), calls=%async_computation.2 | async-start | bytes 17842176 | tf_op jit(solution)/shard_map/reduce_scatter | solution.py:64
  8.0 149.4 %collective-permute-start.11 = (bf16[2816,352]{0,1:T(8,128)(2,1)}, bf16[2816,352]{0,1:T(8,128)(2,1)}, u32[]{:S(2)}, u32[]{:S(2)}) collective-permute-start(bf16[2816,352]{0,1:T(8,128)(2,1)} %param.13), channel_id=1, source_target_pairs={{0,4},{4,0},{8,12},{12,8},{16,20},{20,16},{24,28},{28,24},{1,5},{5... | collective-permute-start | bytes 5947400 | tf_op jit(solution)/shard_map/ppermute | solution.py:14
  45.6 19.4 %collective-permute-start = (bf16[512,704]{0,1:T(8,128)(2,1)}, bf16[512,704]{0,1:T(8,128)(2,1)}, u32[]{:S(2)}, u32[]{:S(2)}) collective-permute-start(bf16[512,704]{0,1:T(8,128)(2,1)} %copy.16), channel_id=1, source_target_pairs={{0,1},{1,0},{2,3},{3,2},{4,5},{5,4},{6,7},{7,6},{8,9},{9,8},{10,11... | collective-permute-start | bytes 2162696 | tf_op jit(solution)/shard_map/ppermute | solution.py:46
  47.5 32.8 %collective-permute-start.3 = (bf16[512,704]{0,1:T(8,128)(2,1)S(1)}, bf16[512,704]{0,1:T(8,128)(2,1)S(1)}, u32[]{:S(2)}, u32[]{:S(2)}) collective-permute-start(bf16[512,704]{0,1:T(8,128)(2,1)S(1)} %copy.22), channel_id=1, source_target_pairs={{0,1},{1,0},{2,3},{3,2},{4,5},{5,4},{6,7},{7,6},{8,9},{9,8},{10,11... | collective-permute-start | bytes 2162696 | tf_op jit(solution)/shard_map/ppermute | solution.py:46
  48.1 72.0 %collective-permute-start.1 = (bf16[512,704]{0,1:T(8,128)(2,1)S(1)}, bf16[512,704]{0,1:T(8,128)(2,1)}, u32[]{:S(2)}, u32[]{:S(2)}) collective-permute-start(bf16[512,704]{0,1:T(8,128)(2,1)S(1)} %copy-done.19), channel_id=1, source_target_pairs={{0,2},{1,3},{2,0},{3,1},{4,6},{5,7},{6,4},{7,5},{8,10},{9,11},{10,... | collective-permute-start | bytes 2162696 | tf_op jit(solution)/shard_map/ppermute | solution.py:46
  48.7 80.5 %collective-permute-start.4 = (bf16[512,704]{0,1:T(8,128)(2,1)S(1)}, bf16[512,704]{0,1:T(8,128)(2,1)}, u32[]{:S(2)}, u32[]{:S(2)}) collective-permute-start(bf16[512,704]{0,1:T(8,128)(2,1)S(1)} %copy.22), channel_id=1, source_target_pairs={{0,2},{1,3},{2,0},{3,1},{4,6},{5,7},{6,4},{7,5},{8,10},{9,11},{10,... | collective-permute-start | bytes 2162696 | tf_op jit(solution)/shard_map/ppermute | solution.py:46
  65.0 73.5 %collective-permute-start.2 = (bf16[512,704]{0,1:T(8,128)(2,1)S(1)}, bf16[512,704]{0,1:T(8,128)(2,1)}, u32[]{:S(2)}, u32[]{:S(2)}) collective-permute-start(bf16[512,704]{0,1:T(8,128)(2,1)S(1)} %copy-done.19), channel_id=1, source_target_pairs={{0,3},{1,2},{2,1},{3,0},{4,7},{5,6},{6,5},{7,4},{8,11},{9,10},{10,... | collective-permute-start | bytes 2162696 | tf_op jit(solution)/shard_map/ppermute | solution.py:46
  80.3 67.5 %collective-permute-start.5 = (bf16[512,704]{0,1:T(8,128)(2,1)S(1)}, bf16[512,704]{0,1:T(8,128)(2,1)}, u32[]{:S(2)}, u32[]{:S(2)}) collective-permute-start(bf16[512,704]{0,1:T(8,128)(2,1)S(1)} %copy.22), channel_id=1, source_target_pairs={{0,3},{1,2},{2,1},{3,0},{4,7},{5,6},{6,5},{7,4},{8,11},{9,10},{10,... | collective-permute-start | bytes 2162696 | tf_op jit(solution)/shard_map/ppermute | solution.py:46
  161.3 80.7 %collective-permute-start.12 = (bf16[2816,704]{0,1:T(8,128)(2,1)}, bf16[2816,704]{0,1:T(8,128)(2,1)}, u32[]{:S(2)}, u32[]{:S(2)}) collective-permute-start(bf16[2816,704]{0,1:T(8,128)(2,1)} %maximum_select_fusion.2), channel_id=1, source_target_pairs={{0,8},{4,12},{8,0},{12,4},{16,24},{20,28},{24,16},{28,20},{1,9},{5... | collective-permute-start | bytes 11894792 | tf_op jit(solution)/shard_map/ppermute | solution.py:14
  196.9 57.6 %collective-permute-start.6 = (bf16[4,352,2816]{2,1,0:T(8,128)(2,1)}, bf16[4,352,2816]{2,1,0:T(8,128)(2,1)}, u32[]{:S(2)}, u32[]{:S(2)}) collective-permute-start(bf16[4,352,2816]{2,1,0:T(8,128)(2,1)} %dynamic-slice_bitcast_fusion), channel_id=1, source_target_pairs={{0,4},{4,0},{8,12},{12,8},{16,20},{20,16},{24,28},{28,24},{1,5},{5... | collective-permute-start | bytes 23789576 | tf_op jit(solution)/shard_map/ppermute | solution.py:75
  252.1 336.7 %collective-permute-start.13 = (bf16[2816,1408]{0,1:T(8,128)(2,1)}, bf16[2816,1408]{0,1:T(8,128)(2,1)}, u32[]{:S(2)}, u32[]{:S(2)}) collective-permute-start(bf16[2816,1408]{0,1:T(8,128)(2,1)} %maximum_select_fusion.1), channel_id=1, source_target_pairs={{0,16},{4,20},{8,24},{12,28},{16,0},{20,4},{24,8},{28,12},{1,17},{... | collective-permute-start | bytes 23789576 | tf_op jit(solution)/shard_map/ppermute | solution.py:14
  265.0 7.0 collective-permute-start.9
  267.0 192.1 %collective-permute-start.7 = (bf16[352,2816]{1,0:T(8,128)(2,1)}, bf16[352,2816]{1,0:T(8,128)(2,1)}, u32[]{:S(2)}, u32[]{:S(2)}) collective-permute-start(bf16[352,2816]{1,0:T(8,128)(2,1)} %get-tuple-element.138), channel_id=1, source_target_pairs={{0,8},{4,12},{1,9},{5,13},{2,10},{6,14},{3,11},{7,15}} | collective-permute-start | bytes 5947400 | tf_op jit(solution)/shard_map/ppermute | solution.py:85
  464.7 139.6 %collective-permute-start.8 = (bf16[352,2816]{1,0:T(8,128)(2,1)}, bf16[352,2816]{1,0:T(8,128)(2,1)}, u32[]{:S(2)}, u32[]{:S(2)}) collective-permute-start(bf16[352,2816]{1,0:T(8,128)(2,1)} %get-tuple-element.136), channel_id=1, source_target_pairs={{0,8},{4,12},{8,16},{12,20},{1,9},{5,13},{9,17},{13,21},{2,10},{6,... | collective-permute-start | bytes 5947400 | tf_op jit(solution)/shard_map/ppermute | solution.py:85
  470.4 134.0 %collective-permute-start.10 = (bf16[352,2816]{1,0:T(8,128)(2,1)}, bf16[352,2816]{1,0:T(8,128)(2,1)}, u32[]{:S(2)}, u32[]{:S(2)}) collective-permute-start(bf16[352,2816]{1,0:T(8,128)(2,1)} %get-tuple-element.135), channel_id=1, source_target_pairs={{28,20},{24,16},{20,12},{16,8},{29,21},{25,17},{21,13},{17,9},{30,... | collective-permute-start | bytes 5947400 | tf_op jit(solution)/shard_map/ppermute | solution.py:86
  653.2 27.5 %collective-permute-start.16 = (bf16[512,704]{0,1:T(8,128)(2,1)}, bf16[512,704]{0,1:T(8,128)(2,1)S(1)}, u32[]{:S(2)}, u32[]{:S(2)}) collective-permute-start(bf16[512,704]{0,1:T(8,128)(2,1)} %copy.32), channel_id=1, source_target_pairs={{0,3},{1,2},{2,1},{3,0},{4,7},{5,6},{6,5},{7,4},{8,11},{9,10},{10,... | collective-permute-start | bytes 2162696 | tf_op jit(solution)/shard_map/ppermute | solution.py:59
  655.7 33.3 %collective-permute-start.15 = (bf16[512,704]{0,1:T(8,128)(2,1)}, bf16[512,704]{0,1:T(8,128)(2,1)}, u32[]{:S(2)}, u32[]{:S(2)}) collective-permute-start(bf16[512,704]{0,1:T(8,128)(2,1)} %copy.30), channel_id=1, source_target_pairs={{0,2},{1,3},{2,0},{3,1},{4,6},{5,7},{6,4},{7,5},{8,10},{9,11},{10,... | collective-permute-start | bytes 2162696 | tf_op jit(solution)/shard_map/ppermute | solution.py:59
  658.1 33.2 %collective-permute-start.14 = (bf16[512,704]{0,1:T(8,128)(2,1)}, bf16[512,704]{0,1:T(8,128)(2,1)}, u32[]{:S(2)}, u32[]{:S(2)}) collective-permute-start(bf16[512,704]{0,1:T(8,128)(2,1)} %copy.28), channel_id=1, source_target_pairs={{0,1},{1,0},{2,3},{3,2},{4,5},{5,4},{6,7},{7,6},{8,9},{9,8},{10,11... | collective-permute-start | bytes 2162696 | tf_op jit(solution)/shard_map/ppermute | solution.py:59
  675.8 28.5 %collective-permute-start.19 = (bf16[512,704]{0,1:T(8,128)(2,1)}, bf16[512,704]{0,1:T(8,128)(2,1)S(1)}, u32[]{:S(2)}, u32[]{:S(2)}) collective-permute-start(bf16[512,704]{0,1:T(8,128)(2,1)} %copy.38), channel_id=1, source_target_pairs={{0,3},{1,2},{2,1},{3,0},{4,7},{5,6},{6,5},{7,4},{8,11},{9,10},{10,... | collective-permute-start | bytes 2162696 | tf_op jit(solution)/shard_map/ppermute | solution.py:59
  678.2 38.3 %collective-permute-start.18 = (bf16[512,704]{0,1:T(8,128)(2,1)}, bf16[512,704]{0,1:T(8,128)(2,1)S(1)}, u32[]{:S(2)}, u32[]{:S(2)}) collective-permute-start(bf16[512,704]{0,1:T(8,128)(2,1)} %copy.36), channel_id=1, source_target_pairs={{0,2},{1,3},{2,0},{3,1},{4,6},{5,7},{6,4},{7,5},{8,10},{9,11},{10,... | collective-permute-start | bytes 2162696 | tf_op jit(solution)/shard_map/ppermute | solution.py:59
  680.7 36.9 %collective-permute-start.17 = (bf16[512,704]{0,1:T(8,128)(2,1)}, bf16[512,704]{0,1:T(8,128)(2,1)S(1)}, u32[]{:S(2)}, u32[]{:S(2)}) collective-permute-start(bf16[512,704]{0,1:T(8,128)(2,1)} %copy.34), channel_id=1, source_target_pairs={{0,1},{1,0},{2,3},{3,2},{4,5},{5,4},{6,7},{7,6},{8,9},{9,8},{10,11... | collective-permute-start | bytes 2162696 | tf_op jit(solution)/shard_map/ppermute | solution.py:59
  748.4 111.9 %copy-start.28 = (f32[704]{0:T(1024)S(1)}, f32[704]{0:T(1024)}, u32[]{:S(2)}) copy-start(f32[704]{0:T(1024)} %copy-done.27) | copy-start | bytes 8452
  748.4 111.9 %copy-start.30 = (f32[704]{0:T(1024)S(1)}, f32[704]{0:T(1024)}, u32[]{:S(2)}) copy-start(f32[704]{0:T(1024)} %copy-done.29) | copy-start | bytes 8452
  748.4 111.9 %copy-start.32 = (f32[704]{0:T(1024)S(1)}, f32[704]{0:T(1024)}, u32[]{:S(2)}) copy-start(f32[704]{0:T(1024)} %copy-done.31) | copy-start | bytes 8452
  748.4 111.9 %copy-start.34 = (f32[704]{0:T(1024)S(1)}, f32[704]{0:T(1024)}, u32[]{:S(2)}) copy-start(f32[704]{0:T(1024)} %copy-done.33) | copy-start | bytes 8452
  748.4 111.9 %copy-start.36 = (f32[704]{0:T(1024)S(1)}, f32[704]{0:T(1024)}, u32[]{:S(2)}) copy-start(f32[704]{0:T(1024)} %copy-done.35) | copy-start | bytes 8452
  748.4 111.9 %copy-start.38 = (f32[704]{0:T(1024)S(1)}, f32[704]{0:T(1024)}, u32[]{:S(2)}) copy-start(f32[704]{0:T(1024)} %copy-done.37) | copy-start | bytes 8452
  748.4 111.9 %copy-start.40 = (f32[704]{0:T(1024)S(1)}, f32[704]{0:T(1024)}, u32[]{:S(2)}) copy-start(f32[704]{0:T(1024)} %copy-done.39) | copy-start | bytes 8452
  748.5 111.9 %copy-start.42 = (f32[704]{0:T(1024)S(1)}, f32[704]{0:T(1024)}, u32[]{:S(2)}) copy-start(f32[704]{0:T(1024)} %copy-done.41) | copy-start | bytes 8452
  748.5 111.9 %copy-start.44 = (f32[704]{0:T(1024)S(1)}, f32[704]{0:T(1024)}, u32[]{:S(2)}) copy-start(f32[704]{0:T(1024)} %copy-done.43) | copy-start | bytes 8452
  748.5 111.9 %copy-start.46 = (f32[704]{0:T(1024)S(1)}, f32[704]{0:T(1024)}, u32[]{:S(2)}) copy-start(f32[704]{0:T(1024)} %copy-done.45) | copy-start | bytes 8452
  748.5 111.9 %copy-start.48 = (f32[704]{0:T(1024)S(1)}, f32[704]{0:T(1024)}, u32[]{:S(2)}) copy-start(f32[704]{0:T(1024)} %copy-done.47) | copy-start | bytes 8452
  748.5 111.9 %copy-start.50 = (f32[704]{0:T(1024)S(1)}, f32[704]{0:T(1024)}, u32[]{:S(2)}) copy-start(f32[704]{0:T(1024)} %copy-done.49) | copy-start | bytes 8452
  748.5 111.9 %copy-start.52 = (f32[704]{0:T(1024)S(1)}, f32[704]{0:T(1024)}, u32[]{:S(2)}) copy-start(f32[704]{0:T(1024)} %copy-done.51) | copy-start | bytes 8452
  748.5 111.9 %copy-start.54 = (f32[704]{0:T(1024)S(1)}, f32[704]{0:T(1024)}, u32[]{:S(2)}) copy-start(f32[704]{0:T(1024)} %copy-done.53) | copy-start | bytes 8452
  748.5 111.9 %copy-start.56 = (f32[704]{0:T(1024)S(1)}, f32[704]{0:T(1024)}, u32[]{:S(2)}) copy-start(f32[704]{0:T(1024)} %copy-done.55) | copy-start | bytes 8452
  748.5 111.9 %copy-start.58 = (f32[704]{0:T(1024)S(1)}, f32[704]{0:T(1024)}, u32[]{:S(2)}) copy-start(f32[704]{0:T(1024)} %copy-done.57) | copy-start | bytes 8452
  748.5 111.9 %copy-start.60 = (f32[704]{0:T(1024)S(1)}, f32[704]{0:T(1024)}, u32[]{:S(2)}) copy-start(f32[704]{0:T(1024)} %copy-done.59) | copy-start | bytes 8452
  748.6 111.9 %copy-start.62 = (f32[704]{0:T(1024)S(1)}, f32[704]{0:T(1024)}, u32[]{:S(2)}) copy-start(f32[704]{0:T(1024)} %copy-done.61) | copy-start | bytes 8452
  748.6 111.9 %copy-start.64 = (f32[704]{0:T(1024)S(1)}, f32[704]{0:T(1024)}, u32[]{:S(2)}) copy-start(f32[704]{0:T(1024)} %copy-done.63) | copy-start | bytes 8452
  748.6 111.9 %copy-start.66 = (f32[704]{0:T(1024)S(1)}, f32[704]{0:T(1024)}, u32[]{:S(2)}) copy-start(f32[704]{0:T(1024)} %copy-done.65) | copy-start | bytes 8452
  748.6 111.9 %copy-start.68 = (f32[704]{0:T(1024)S(1)}, f32[704]{0:T(1024)}, u32[]{:S(2)}) copy-start(f32[704]{0:T(1024)} %copy-done.67) | copy-start | bytes 8452
  748.6 111.9 %copy-start.70 = (f32[704]{0:T(1024)S(1)}, f32[704]{0:T(1024)}, u32[]{:S(2)}) copy-start(f32[704]{0:T(1024)} %copy-done.69) | copy-start | bytes 8452
  748.6 111.9 %copy-start.72 = (f32[704]{0:T(1024)S(1)}, f32[704]{0:T(1024)}, u32[]{:S(2)}) copy-start(f32[704]{0:T(1024)} %copy-done.71) | copy-start | bytes 8452
  748.6 111.9 %copy-start.74 = (f32[704]{0:T(1024)S(1)}, f32[704]{0:T(1024)}, u32[]{:S(2)}) copy-start(f32[704]{0:T(1024)} %copy-done.73) | copy-start | bytes 8452
  748.6 111.9 %copy-start.76 = (f32[704]{0:T(1024)S(1)}, f32[704]{0:T(1024)}, u32[]{:S(2)}) copy-start(f32[704]{0:T(1024)} %copy-done.75) | copy-start | bytes 8452
  748.6 111.9 %copy-start.78 = (f32[704]{0:T(1024)S(1)}, f32[704]{0:T(1024)}, u32[]{:S(2)}) copy-start(f32[704]{0:T(1024)} %copy-done.77) | copy-start | bytes 8452
  748.6 111.9 %copy-start.80 = (f32[704]{0:T(1024)S(1)}, f32[704]{0:T(1024)}, u32[]{:S(2)}) copy-start(f32[704]{0:T(1024)} %copy-done.79) | copy-start | bytes 8452
  748.7 111.9 %copy-start.82 = (f32[704]{0:T(1024)S(1)}, f32[704]{0:T(1024)}, u32[]{:S(2)}) copy-start(f32[704]{0:T(1024)} %copy-done.81) | copy-start | bytes 8452
  748.7 111.9 %copy-start.84 = (f32[704]{0:T(1024)S(1)}, f32[704]{0:T(1024)}, u32[]{:S(2)}) copy-start(f32[704]{0:T(1024)} %copy-done.83) | copy-start | bytes 8452
  748.7 111.9 %copy-start.86 = (f32[704]{0:T(1024)S(1)}, f32[704]{0:T(1024)}, u32[]{:S(2)}) copy-start(f32[704]{0:T(1024)} %copy-done.85) | copy-start | bytes 8452
  748.7 111.9 %copy-start.88 = (f32[704]{0:T(1024)S(1)}, f32[704]{0:T(1024)}, u32[]{:S(2)}) copy-start(f32[704]{0:T(1024)} %copy-done.87) | copy-start | bytes 8452
  748.7 111.9 %copy-start.90 = (f32[704]{0:T(1024)S(1)}, f32[704]{0:T(1024)}, u32[]{:S(2)}) copy-start(f32[704]{0:T(1024)} %copy-done.89) | copy-start | bytes 8452
  748.7 111.9 %copy-start.92 = (f32[704]{0:T(1024)S(1)}, f32[704]{0:T(1024)}, u32[]{:S(2)}) copy-start(f32[704]{0:T(1024)} %copy-done.91) | copy-start | bytes 8452
  748.7 111.9 %copy-start.94 = (f32[704]{0:T(1024)S(1)}, f32[704]{0:T(1024)}, u32[]{:S(2)}) copy-start(f32[704]{0:T(1024)} %copy-done.93) | copy-start | bytes 8452
  748.7 111.9 %copy-start.96 = (f32[704]{0:T(1024)S(1)}, f32[704]{0:T(1024)}, u32[]{:S(2)}) copy-start(f32[704]{0:T(1024)} %copy-done.95) | copy-start | bytes 8452
  748.7 111.9 %copy-start.98 = (f32[704]{0:T(1024)S(1)}, f32[704]{0:T(1024)}, u32[]{:S(2)}) copy-start(f32[704]{0:T(1024)} %copy-done.97) | copy-start | bytes 8452
  748.7 111.9 %copy-start.100 = (f32[704]{0:T(1024)S(1)}, f32[704]{0:T(1024)}, u32[]{:S(2)}) copy-start(f32[704]{0:T(1024)} %copy-done.99) | copy-start | bytes 8452
  748.8 33.5 %collective-permute-start.20 = (f32[52,704]{1,0:T(8,128)S(1)}, f32[52,704]{1,0:T(8,128)S(1)}, u32[]{:S(2)}, u32[]{:S(2)}) collective-permute-start(f32[52,704]{1,0:T(8,128)S(1)} %pad_maximum_fusion), channel_id=1, source_target_pairs={{0,4},{4,0},{8,12},{12,8},{16,20},{20,16},{24,28},{28,24},{1,5},{5... | collective-permute-start | bytes 439304 | tf_op jit(solution)/shard_map/ppermute | solution.py:97
  754.7 120.6 %collective-permute-start.24 = (bf16[352,2816]{1,0:T(8,128)(2,1)}, bf16[352,2816]{1,0:T(8,128)(2,1)}, u32[]{:S(2)}, u32[]{:S(2)}) collective-permute-start(bf16[352,2816]{1,0:T(8,128)(2,1)} %get-tuple-element.134), channel_id=1, source_target_pairs={{28,20},{24,16},{20,12},{16,8},{12,4},{8,0},{29,21},{25,17},{21,13... | collective-permute-start | bytes 5947400 | tf_op jit(solution)/shard_map/ppermute | solution.py:86
  756.1 119.2 %collective-permute-start.23 = (bf16[352,2816]{1,0:T(8,128)(2,1)}, bf16[352,2816]{1,0:T(8,128)(2,1)}, u32[]{:S(2)}, u32[]{:S(2)}) collective-permute-start(bf16[352,2816]{1,0:T(8,128)(2,1)} %get-tuple-element.133), channel_id=1, source_target_pairs={{0,8},{4,12},{8,16},{12,20},{16,24},{20,28},{1,9},{5,13},{9,17},{1... | collective-permute-start | bytes 5947400 | tf_op jit(solution)/shard_map/ppermute | solution.py:85
  782.3 75.9 %collective-permute-start.21 = (f32[52,704]{1,0:T(8,128)S(1)}, f32[52,704]{1,0:T(8,128)S(1)}, u32[]{:S(2)}, u32[]{:S(2)}) collective-permute-start(f32[52,704]{1,0:T(8,128)S(1)} %fusion.123), channel_id=1, source_target_pairs={{0,8},{4,12},{8,0},{12,4},{16,24},{20,28},{24,16},{28,20},{1,9},{5... | collective-permute-start | bytes 439304 | tf_op jit(solution)/shard_map/ppermute | solution.py:97
  858.2 15.7 %collective-permute-start.22 = (f32[52,704]{1,0:T(8,128)S(1)}, f32[52,704]{1,0:T(8,128)S(1)}, u32[]{:S(2)}, u32[]{:S(2)}) collective-permute-start(f32[52,704]{1,0:T(8,128)S(1)} %add.568), channel_id=1, source_target_pairs={{0,16},{4,20},{8,24},{12,28},{16,0},{20,4},{24,8},{28,12},{1,17},{... | collective-permute-start | bytes 439304 | tf_op jit(solution)/shard_map/ppermute | solution.py:97
  (71 other events, 1026.3 us)
Sparse Core Ops, SparseCore 0:
  9.7 146.2 all-gather.1
  635.8 208.0 reduce-scatter.1
